TPU v7x, 32 devices: a whole 2x2x4 slice. The times are simulated.
32 devices in a mesh: fsdp: 8 (over z, y), tp: 4 (over x, core).
Axes of the slice: x: 2, y: 2, z: 4, core: 2. Of those that a mesh axis runs over, the one named last changes fastest.
Arguments:
- grads: bfloat16 [8, 2, 4096, 2048], P('fsdp', None, 'tp'), may hold values from -144 to 144
- master: float32 [4096, 2048], P('tp', 'fsdp'), may hold values from -0.3125 to 0.3125
- moment: float32 [4096, 2048], P('tp', 'fsdp'), may hold values from -1.5 to 1.5
- second: float32 [4096, 2048], P('tp', 'fsdp'), may hold values from 0.02 to 0.3
- stats: float32 [4, 1024, 1024], P('tp', 'fsdp'), may hold values from -0.05 to 0.35
- basis: float32 [4, 1024, 1024], P('tp', 'fsdp'), may hold values from -0.5 to 1.5
Outputs:
- weights: bfloat16 [4096, 2048], P('tp')
- master_new: float32 [4096, 2048], P('tp', 'fsdp')
- moment_new: float32 [4096, 2048], P('tp', 'fsdp')
- second_new: float32 [4096, 2048], P('tp', 'fsdp')
- stats_new: float32 [4, 1024, 1024], P('tp', 'fsdp')
- basis_new: float32 [4, 1024, 1024], P('tp', 'fsdp')
All inputs are finite; a program needn't handle non-finite values.
Results may differ from a plain program's by a relative error of at most 0.007.
Values may be sent and summed in bfloat16 or wider, within the bound.
A program may use at most 128 MiB of HBM per device.

v0:
```python
import jax
import jax.numpy as jnp
from jax import lax
from jax.sharding import PartitionSpec as P

D = 4096
KVW = 2048
poly_first = 3.4445
poly_second = -4.775
poly_third = 2.0315
bf16 = jnp.bfloat16
f32 = jnp.float32


def exact(a, b):
    return jnp.dot(a, b, precision=lax.Precision.HIGHEST)


def split(a):
    top = a.astype(bf16)
    return (top, (a - top.astype(f32)).astype(bf16))


def three(a, b):
    a_top, a_low = split(a)
    b_top, b_low = split(b)
    mm = lambda u, v: jnp.dot(u, v, preferred_element_type=f32)
    return mm(a_top, b_top) + (mm(a_low, b_top) + mm(a_top, b_low))


def body(grads, master, moment, second, stats, basis):
    n = lax.axis_size("fsdp")
    rows = master.shape[0]
    cols = master.shape[1]
    own_rows = basis[0]
    stat_rows = stats[0]
    whole = lax.all_gather(own_rows.astype(bf16), "fsdp", axis=0, tiled=True)
    local = jnp.sum(grads.astype(f32), axis=(0, 1)).astype(bf16)
    pieces = lax.all_to_all(local, "fsdp", split_axis=1, concat_axis=0, tiled=True)
    summed = jnp.sum(pieces.reshape(n, rows, cols).astype(f32), axis=0)
    squares = jnp.sum(lax.all_gather(jnp.sum(summed * summed).reshape(1), ("fsdp", "tp")))
    ratio = jnp.minimum(1.0, jnp.sqrt(float(D * KVW) / (squares + 1e-06)))
    total = summed.astype(bf16)
    part = jnp.dot(total, total.T, preferred_element_type=f32).astype(bf16)
    strips = lax.all_to_all(part, "fsdp", split_axis=0, concat_axis=0, tiled=True)
    outer = jnp.sum(strips.reshape(n, rows // n, rows).astype(f32), axis=0) * (ratio * ratio)
    stats_new = 0.9 * stat_rows + 0.1 / KVW * outer
    s_top, s_low = split(stats_new)
    power = jnp.dot(s_top, whole, preferred_element_type=f32) + jnp.dot(
        s_low, whole, preferred_element_type=f32
    )
    every = lax.all_gather(power.astype(bf16), "fsdp", axis=0, tiled=True)
    rotated = jnp.dot(whole.T, total, preferred_element_type=f32) * ratio
    moment_new = 0.9 * moment + 0.1 * rotated
    second_new = 0.95 * second + 0.05 * rotated * rotated
    update = moment_new / (jnp.sqrt(second_new) + 1e-08)
    delta = jnp.dot(whole, update.astype(bf16), preferred_element_type=f32)
    master_new = master - 0.01 * (delta + 0.1 * master)
    weights = lax.all_gather(master_new.astype(bf16), "fsdp", axis=1, tiled=True)
    raw = jnp.dot(every.T, every, preferred_element_type=f32)
    diag = lax.broadcasted_iota(jnp.int32, (rows, rows), 0) == lax.broadcasted_iota(
        jnp.int32, (rows, rows), 1
    )
    norm = 1.0 / jnp.sqrt(jnp.sum(jnp.where(diag, raw, 0.0)) + 1e-06)
    gram = raw * (norm * norm)
    current = power * norm
    mixed = jnp.where(diag, poly_first, 0.0) + poly_second * gram + poly_third * three(gram, gram)
    current = three(current, mixed)
    gram = three(mixed, three(mixed, gram))
    product = three(current, gram)
    current = poly_first * current + poly_second * product + poly_third * three(product, gram)
    return (weights, master_new, moment_new, second_new, stats_new[None], current[None])


def solution(mesh):
    in_specs = (
        P("fsdp", None, "tp", None),
        P("tp", "fsdp"),
        P("tp", "fsdp"),
        P("tp", "fsdp"),
        P("tp", "fsdp", None),
        P("tp", "fsdp", None),
    )
    out_specs = (
        P("tp", None),
        P("tp", "fsdp"),
        P("tp", "fsdp"),
        P("tp", "fsdp"),
        P("tp", "fsdp", None),
        P("tp", "fsdp", None),
    )
    return jax.shard_map(body, mesh=mesh, in_specs=in_specs, out_specs=out_specs, check_vma=False)
```

profile of v0, /device:TPU:0, one launch (start us, length us, event | category | flops | bytes accessed | tf_op | source)
XLA Modules:
  0.0 366.2 jit_solution(5923313504358977901)
XLA Ops:
  7.2 8.8 %reduce_sum.57 = bf16[1024,2048]{1,0:T(8,128)(2,1)} reduce(bf16[1,2,1024,2048]{3,2,1,0:T(8,128)(2,1)} %param.6, bf16[]{:T(256)} %constant.16.clone.1), dimensions={0,1}, to_apply=%region_0.0 | reduce | flops 2097152 | bytes 12582914 | tf_op jit(solution)/shard_map/reduce_sum | solution.py:38
  16.0 6.4 %copy.48 = bf16[1024,2048]{0,1:T(8,128)(2,1)} copy(bf16[1024,2048]{1,0:T(8,128)(2,1)} %reduce_sum.57) | data formatting | bytes 8388608 | tf_op jit(solution)/shard_map/reduce_sum | solution.py:38
  22.3 6.4 %copy.49 = bf16[1024,8,256]{2,0,1:T(8,128)(2,1)} copy(bf16[1024,8,256]{0,2,1:T(8,128)(2,1)} %bitcast.79) | data formatting | bytes 8388608 | tf_op jit(solution)/shard_map/all_to_all | solution.py:39
  28.8 100.5 %all_to_all.22 = bf16[1024,8,256]{2,0,1:T(8,128)(2,1)S(1)} all-to-all(bf16[1024,8,256]{2,0,1:T(8,128)(2,1)} %copy.49), channel_id=1, replica_groups=mesh['fsdp'=8,'tp'=4] {'fsdp'}, dimensions={1} | all-to-all | bytes 8388608 | tf_op jit(solution)/shard_map/all_to_all | solution.py:39
  131.9 3.6 all-to-all-start.1
  139.0 84.3 %all-reduce = f32[32]{0:T(128)S(1)} all-reduce(f32[32]{0:T(128)S(1)} %dynamic-update-slice), channel_id=1, replica_groups=mesh['fsdp'=8,'tp'=4] {'fsdp','tp'}, use_global_device_ids=true, to_apply=%add | all-reduce | flops 32 | bytes 256
  225.8 2.5 fusion.1
  230.2 2.5 copy.47
  232.8 2.5 copy.50
  235.3 2.5 copy.52
  237.8 3.8 %fusion.36 = (f32[1024,256]{0,1:T(8,128)}, f32[1024,256]{0,1:T(8,128)}) fusion(f32[1024,256]{0,1:T(8,128)} %copy.50, f32[1024,256]{0,1:T(8,128)} %copy.47, f32[]{:T(128)S(6)} %min.3, bf16[1,1024,1024]{2,1,0:T(8,128)(2,1)S(1)} %copy-done, f32[1024,256]{1,0:T(8,128)S(1)} %convert_reduce_fusion), kind=kOutput, calls=%fused_computation.39 | convolution fusion | flops 539230208 | bytes 7340036 | tf_op jit(solution)/shard_map/dot_general | solution.py:53
  241.7 2.6 copy.55
  245.6 3.6 fusion.71
  249.2 2.6 copy.54
  252.8 26.4 %all-gather.7.cloned.1.call-done = bf16[1024,1024]{1,0:T(8,128)(2,1)} async-done(((bf16[128,1024]{1,0:T(8,128)(2,1)}), bf16[1024,1024]{1,0:T(8,128)(2,1)}) %all-gather.7.cloned.1.call-update) | async-done | bytes 2097168 | tf_op jit(solution)/shard_map/all_gather | solution.py:52
  279.2 7.2 %select_reduce_fusion = (f32[]{:T(128)}, f32[1024,1024]{1,0:T(8,128)}) fusion(bf16[1024,1024]{1,0:T(8,128)(2,1)} %all-gather.7.cloned.1.call-done), kind=kOutput, calls=%fused_computation.8 | convolution fusion | flops 2150629376 | bytes 6291460 | tf_op jit(solution)/shard_map/dot_general | solution.py:60
  287.1 3.3 subtract_convert_fusion.3
  295.2 3.2 subtract_convert_fusion.2
  304.4 2.6 add_add_fusion.1
  307.0 2.3 fusion.54
  309.4 2.3 fusion
  311.7 2.4 add_add_fusion
  317.8 35.5 %all-gather.5.cloned.1.call-done = bf16[1024,2048]{0,1:T(8,128)(2,1)} async-done(((bf16[1024,256]{0,1:T(8,128)(2,1)}), bf16[1024,2048]{0,1:T(8,128)(2,1)}) %all-gather.5.cloned.1.call-update) | async-done | bytes 4194320 | tf_op jit(solution)/shard_map/all_gather | solution.py:59
  353.2 6.4 %copy.53 = bf16[1024,2048]{1,0:T(8,128)(2,1)} copy(bf16[1024,2048]{0,1:T(8,128)(2,1)} %all-gather.5.cloned.1.call-done) | data formatting | bytes 8388608
  (48 shorter events, 26.3 us)
Async XLA Ops:
  131.9 92.8 %all-to-all-start.1 = ((bf16[8,128,1024]{2,1,0:T(8,128)(2,1)}), bf16[8,128,1024]{2,1,0:T(8,128)(2,1)S(1)}, u32[]{:S(2)}, u32[]{:S(2)}) async-start(bf16[8,128,1024]{2,1,0:T(8,128)(2,1)} %bitcast.80), calls=%async_computation.1 | async-start | bytes 4194304 | tf_op jit(solution)/shard_map/all_to_all | solution.py:45
  135.5 90.3 %all-gather.9.cloned.1.call-start = ((), (), s32[]{:S(2)}) async-start(), calls=%async_computation.4 | async-start | bytes 2359296 | tf_op jit(solution)/shard_map/all_gather | solution.py:37
  137.3 141.9 %all-gather.7.cloned.1.call-start = ((), (), s32[]{:S(2)}) async-start(), calls=%async_computation.3 | async-start | bytes 2359296 | tf_op jit(solution)/shard_map/all_gather | solution.py:52
  225.8 2.5 copy-start
  225.8 2.6 copy-start.1
  225.8 2.8 copy-start.4
  230.0 123.2 %all-gather.5.cloned.1.call-start = ((), (), s32[]{:S(2)}) async-start(), calls=%async_computation.2 | async-start | bytes 4718592 | tf_op jit(solution)/shard_map/all_gather | solution.py:59
  241.7 2.6 copy-start.7
  249.2 2.6 copy-start.2
  249.2 2.7 copy-start.5
  292.8 2.4 copy-start.6
  295.2 3.2 copy-start.3
Sparse Core Ops, SparseCore 0:
  139.0 70.8 all-gather.8
  230.1 49.0 all-gather.6
  281.3 71.8 all-gather.4
where the time goes:
time: 367 us; the launch traced here: 366 us
  blocking collectives  185 us (50%)
  waiting for transfers between devices  62 us (17%)
  matrix products  47.8 us (13%)
  local copies, waits for them, and re-layouts  34.4 us (9%)
  other arithmetic  18 us (5%)
  between operations  15.4 us (4%)
  starting transfers between devices  3.91 us (1%)
    all_to_all x1, blocking collectives, body(): lax.all_to_all(local, 'fsdp', split_axis=1, concat_axis=0, tiled=True)  100 us
    unnamed x1, blocking collectives  84.3 us
    all_gather x1, waiting for transfers between devices, body(): lax.all_gather(master_new.astype(bf16), 'fsdp', axis=1, tiled=True)  35.5 us
    dot_general x18, matrix products, three(): mm = lambda u, v: jnp.dot(u, v, preferred_element_type=f32)  27.2 us
    all_gather x1, waiting for transfers between devices, body(): every = lax.all_gather(power.astype(bf16), 'fsdp', axis=0, tiled=True)  26.4 us
    unnamed x25, local copies, waits for them, and re-layouts  21.6 us
    reduce_sum x1, other arithmetic, body(): local = jnp.sum(grads.astype(f32), axis=(0, 1)).astype(bf16)  8.78 us
  transfers between devices with their start and end apart: 4, of which 2 were waited for; matrix products, arithmetic and copies ran while one was open for 18% of the time, Pallas kernels for 0%

commit v1 on v0

--- a/solution.py
+++ b/solution.py
@@ -36,7 +36,10 @@
     stat_rows = stats[0]
     whole = lax.all_gather(own_rows.astype(bf16), "fsdp", axis=0, tiled=True)
     local = jnp.sum(grads.astype(f32), axis=(0, 1)).astype(bf16)
-    pieces = lax.all_to_all(local, "fsdp", split_axis=1, concat_axis=0, tiled=True)
+    pieces = jnp.concatenate(
+        lax.all_to_all(jnp.stack(jnp.split(local, lax.axis_size("fsdp"), axis=1)), "fsdp", 0, 0),
+        axis=0,
+    )
     summed = jnp.sum(pieces.reshape(n, rows, cols).astype(f32), axis=0)
     squares = jnp.sum(lax.all_gather(jnp.sum(summed * summed).reshape(1), ("fsdp", "tp")))
     ratio = jnp.minimum(1.0, jnp.sqrt(float(D * KVW) / (squares + 1e-06)))

time: 367 us -> 364 us (level)
    unnamed x25 -> x26, local copies, waits for them, and re-layouts: 21.6 us -> 29.9 us
    all_to_all x1 -> x0, local copies, waits for them, and re-layouts: 6.42 us -> none  [body(): lax.all_to_all(local, 'fsdp', split_axis=1, concat_axis=0, tiled=True)]
    reduce_sum x1 -> x0, local copies, waits for them, and re-layouts: 6.39 us -> none  [body(): local = jnp.sum(grads.astype(f32), axis=(0, 1)).astype(bf16)]
where the time goes in v1:
time: 364 us; the launch traced here: 363 us
  blocking collectives  185 us (51%)
  waiting for transfers between devices  60.6 us (17%)
  matrix products  49.5 us (14%)
  local copies, waits for them, and re-layouts  31 us (9%)
  other arithmetic  18 us (5%)
  between operations  15.4 us (4%)
  starting transfers between devices  3.91 us (1%)
    all_to_all x1, blocking collectives, body(): lax.all_to_all(jnp.stack(jnp.split(local, lax.axis_size('fsdp'), axis=1))...  100 us
    unnamed x1, blocking collectives  84.3 us
    all_gather x1, waiting for transfers between devices, body(): lax.all_gather(master_new.astype(bf16), 'fsdp', axis=1, tiled=True)  35.5 us
    unnamed x26, local copies, waits for them, and re-layouts  29.9 us
    dot_general x18, matrix products, three(): mm = lambda u, v: jnp.dot(u, v, preferred_element_type=f32)  27.1 us
    all_gather x1, waiting for transfers between devices, body(): every = lax.all_gather(power.astype(bf16), 'fsdp', axis=0, tiled=True)  25.1 us
    reduce_sum x1, other arithmetic, body(): local = jnp.sum(grads.astype(f32), axis=(0, 1)).astype(bf16)  8.78 us
  transfers between devices with their start and end apart: 4, of which 2 were waited for; matrix products, arithmetic and copies ran while one was open for 18% of the time, Pallas kernels for 0%

profile of v1, /device:TPU:0, one launch (start us, length us, event | category | flops | bytes accessed | tf_op | source)
XLA Modules:
  0.0 363.0 jit_solution(7728459106254674096)
XLA Ops:
  7.2 8.8 %reduce_sum.57 = bf16[1024,2048]{1,0:T(8,128)(2,1)} reduce(bf16[1,2,1024,2048]{3,2,1,0:T(8,128)(2,1)} %param.6, bf16[]{:T(256)} %constant.16.clone.1), dimensions={0,1}, to_apply=%region_0.0 | reduce | flops 2097152 | bytes 12582914 | tf_op jit(solution)/shard_map/reduce_sum | solution.py:38
  24.6 100.3 %all_to_all.14 = bf16[8,1024,256]{2,1,0:T(8,128)(2,1)S(1)} all-to-all(bf16[8,1024,256]{2,1,0:T(8,128)(2,1)S(1)} %fusion.37), channel_id=1, replica_groups=mesh['fsdp'=8,'tp'=4] {'fsdp'}, dimensions={0} | all-to-all | bytes 8388608 | tf_op jit(solution)/shard_map/all_to_all | solution.py:40
  127.5 3.6 all-to-all-start.1
  134.7 84.3 %all-reduce = f32[32]{0:T(128)S(1)} all-reduce(f32[32]{0:T(128)S(1)} %dynamic-update-slice), channel_id=1, replica_groups=mesh['fsdp'=8,'tp'=4] {'fsdp','tp'}, use_global_device_ids=true, to_apply=%add | all-reduce | flops 32 | bytes 256
  221.4 2.5 fusion.1
  224.0 2.6 fusion.80
  226.9 2.5 copy.20
  229.4 2.5 copy.21
  231.9 2.5 copy.23
  234.5 3.8 %fusion.36 = (f32[1024,256]{0,1:T(8,128)}, f32[1024,256]{0,1:T(8,128)}) fusion(f32[1024,256]{0,1:T(8,128)} %copy.21, f32[1024,256]{0,1:T(8,128)} %copy.20, f32[]{:T(128)S(6)} %min.3, bf16[1,1024,1024]{2,1,0:T(8,128)(2,1)S(1)} %copy-done, f32[1024,256]{1,0:T(8,128)S(1)} %convert_reduce_fusion), kind=kOutput, calls=%fused_computation.39 | convolution fusion | flops 539230208 | bytes 7340036 | tf_op jit(solution)/shard_map/dot_general | solution.py:56
  238.3 2.5 copy.26
  240.8 2.5 copy.27
  243.4 4.1 %fusion.79 = (bf16[1024,256]{0,1:T(8,128)(2,1)}, f32[1024,256]{0,1:T(8,128)}) fusion(f32[1024,256]{0,1:T(8,128)} %copy.23, bf16[1,1024,1024]{2,1,0:T(8,128)(2,1)S(1)} %copy-done, f32[1024,256]{0,1:T(8,128)} %get-tuple-element.23, f32[1024,256]{0,1:T(8,128)} %get-tuple-element.22), kind=kOutput, calls=%fused_computation.99 | convolution fusion | flops 538968064 | bytes 6815744 | tf_op jit(solution)/shard_map/dot_general | solution.py:60
  247.4 2.5 copy.25
  250.9 25.1 %all-gather.7.cloned.1.call-done = bf16[1024,1024]{1,0:T(8,128)(2,1)} async-done(((bf16[128,1024]{1,0:T(8,128)(2,1)}), bf16[1024,1024]{1,0:T(8,128)(2,1)}) %all-gather.7.cloned.1.call-update) | async-done | bytes 2097168 | tf_op jit(solution)/shard_map/all_gather | solution.py:55
  276.0 7.2 %select_reduce_fusion = (f32[]{:T(128)}, f32[1024,1024]{1,0:T(8,128)}) fusion(bf16[1024,1024]{1,0:T(8,128)(2,1)} %all-gather.7.cloned.1.call-done), kind=kOutput, calls=%fused_computation.8 | convolution fusion | flops 2150629376 | bytes 6291460 | tf_op jit(solution)/shard_map/dot_general | solution.py:63
  283.9 3.3 subtract_convert_fusion.3
  292.0 3.2 subtract_convert_fusion.2
  301.2 2.5 add_add_fusion.1
  303.8 2.3 fusion.62
  306.1 2.4 fusion
  308.5 2.4 add_add_fusion
  314.5 35.5 %all-gather.5.cloned.1.call-done = bf16[1024,2048]{0,1:T(8,128)(2,1)} async-done(((bf16[1024,256]{0,1:T(8,128)(2,1)}), bf16[1024,2048]{0,1:T(8,128)(2,1)}) %all-gather.5.cloned.1.call-update) | async-done | bytes 4194320 | tf_op jit(solution)/shard_map/all_gather | solution.py:62
  350.0 6.4 %copy.24 = bf16[1024,2048]{1,0:T(8,128)(2,1)} copy(bf16[1024,2048]{0,1:T(8,128)(2,1)} %all-gather.5.cloned.1.call-done) | data formatting | bytes 8388608
  (48 shorter events, 32.0 us)
Async XLA Ops:
  127.5 92.8 %all-to-all-start.1 = ((bf16[8,128,1024]{2,1,0:T(8,128)(2,1)}), bf16[8,128,1024]{2,1,0:T(8,128)(2,1)S(1)}, u32[]{:S(2)}, u32[]{:S(2)}) async-start(bf16[8,128,1024]{2,1,0:T(8,128)(2,1)} %bitcast.110), calls=%async_computation.1 | async-start | bytes 4194304 | tf_op jit(solution)/shard_map/all_to_all | solution.py:48
  131.1 90.3 %all-gather.9.cloned.1.call-start = ((), (), s32[]{:S(2)}) async-start(), calls=%async_computation.4 | async-start | bytes 2359296 | tf_op jit(solution)/shard_map/all_gather | solution.py:37
  133.0 143.0 %all-gather.7.cloned.1.call-start = ((), (), s32[]{:S(2)}) async-start(), calls=%async_computation.3 | async-start | bytes 2359296 | tf_op jit(solution)/shard_map/all_gather | solution.py:55
  221.4 2.5 copy-start
  226.6 123.4 %all-gather.5.cloned.1.call-start = ((), (), s32[]{:S(2)}) async-start(), calls=%async_computation.2 | async-start | bytes 4718592 | tf_op jit(solution)/shard_map/all_gather | solution.py:62
  243.4 6.6 %copy-start.1 = (f32[128,1024]{1,0:T(8,128)S(1)}, f32[128,1024]{1,0:T(8,128)}, u32[]{:S(2)}) copy-start(f32[128,1024]{1,0:T(8,128)} %convert_reduce_fusion.1) | copy-start | bytes 1572868
  243.4 6.6 %copy-start.3 = (f32[1,128,1024]{2,1,0:T(8,128)S(1)}, f32[1,128,1024]{2,1,0:T(8,128)}, u32[]{:S(2)}) copy-start(f32[1,128,1024]{2,1,0:T(8,128)} %param.10) | copy-start | bytes 1572868
  289.6 2.4 copy-start.4
  292.0 3.2 copy-start.2
Sparse Core Ops, SparseCore 0:
  134.7 70.8 all-gather.8
  226.8 49.1 all-gather.6
  278.1 71.8 all-gather.4
